TPU v7x, 32 devices: a whole 2x2x4 slice. The times are simulated.
32 devices in a mesh: grp: 4 (over z), shard: 8 (over y, x, core).
Axes of the slice: x: 2, y: 2, z: 4, core: 2. Of those that a mesh axis runs over, the one named last changes fastest.
Arguments:
- frames_in: float32 [128, 256, 768], P(('grp', 'shard')), may hold values from -6 to 6
- cotangent: float32 [128, 256, 768], P(('grp', 'shard')), may hold values from -6 to 6
- time_table: bfloat16 [1000, 768], P(None, 'shard'), may hold values from -6 to 6
- ada_weight: bfloat16 [768, 6912], P('shard'), may hold values from -0.21875 to 0.21875
- ada_bias: bfloat16 [6912], P('shard'), may hold values from -4 to 4
- space_qkv: bfloat16 [768, 2304], P('shard'), may hold values from -0.21875 to 0.21875
- space_out: bfloat16 [768, 768], P('shard'), may hold values from -2.5 to 2.5
- time_qkv: bfloat16 [768, 2304], P('shard'), may hold values from -0.21875 to 0.21875
- time_out: bfloat16 [768, 768], P('shard'), may hold values from -0.875 to 0.875
- up_weight: bfloat16 [768, 3072], P('shard'), may hold values from -0.21875 to 0.21875
- up_bias: bfloat16 [3072], P('shard'), may hold values from -6 to 6
- down_weight: bfloat16 [3072, 768], P('shard'), may hold values from -0.109375 to 0.109375
- down_bias: bfloat16 [768], P('shard'), may hold values from -4 to 4
- timesteps: int32 [8], P('grp'), may hold values from 0 to 999
- task_mask: int32 [8, 16], P('grp'), may hold values 0 or 1
- clip_weight: float32 [8], P('grp'), may hold values from 0.5 to 2
- frame_table: int32 [4, 32], P('grp'), may hold values from 0 to 31, each once within a row
Outputs:
- frames_out: float32 [128, 256, 768], P(('grp', 'shard'))
- grad_frames_in: float32 [128, 256, 768], P(('grp', 'shard'))
- grad_time_table: float32 [1000, 768], P(None, 'shard')
- grad_ada_weight: float32 [768, 6912], P('shard')
- grad_ada_bias: float32 [6912], P('shard')
- grad_space_qkv: float32 [768, 2304], P('shard')
- grad_space_out: float32 [768, 768], P('shard')
- grad_time_qkv: float32 [768, 2304], P('shard')
- grad_time_out: float32 [768, 768], P('shard')
- grad_up_weight: float32 [768, 3072], P('shard')
- grad_up_bias: float32 [3072], P('shard')
- grad_down_weight: float32 [3072, 768], P('shard')
- grad_down_bias: float32 [768], P('shard')
Inputs may be any that keep to these rules, and one draw needn't show every extreme that they name: `frame_table`: each row lists every frame of its group once.
All inputs are finite; a program needn't handle non-finite values. No bound on the sum of `task_mask` on one device may be relied on, other than what follows from the above.
Results may differ from a plain program's by a relative error of at most 0.014.
Values may be sent and summed in bfloat16 or wider, within the bound.
No kernel may reach another device: no remote copies, remote signals or barrier semaphores. Data moves between devices by JAX's collectives and lax.ppermute only.
A program may use at most 256 MiB of HBM per device.

v0:
```python
from functools import partial
import jax
import jax.numpy as jnp
from jax import lax
from jax.sharding import PartitionSpec as P

HEADS = 12
HEAD_DIM = 64
HIGH = lax.Precision.HIGHEST
EPSILON = 1e-06


def layer_norm(values):
    center = values - jnp.mean(values, axis=-1, keepdims=True)
    spread = jnp.mean(center * center, axis=-1, keepdims=True)
    inverse = lax.rsqrt(spread + EPSILON)
    return (center * inverse, inverse)


def norm_back(grad_normed, normed, inverse):
    first = jnp.mean(grad_normed, axis=-1, keepdims=True)
    second = jnp.mean(grad_normed * normed, axis=-1, keepdims=True)
    return inverse * (grad_normed - first - normed * second)


def split_heads(packed, width):
    shape = packed.shape[:-1] + (HEADS, HEAD_DIM)
    return (
        packed[..., :width].reshape(shape),
        packed[..., width : 2 * width].reshape(shape),
        packed[..., 2 * width :].reshape(shape),
    )


def attend_forward(packed):
    width = packed.shape[-1] // 3
    query, keys, values = split_heads(packed, width)
    scores = jnp.einsum(
        "blmhe,bkmhe->bmhlk", query, keys, preferred_element_type=jnp.float32
    ) * HEAD_DIM ** (-0.5)
    highest = jnp.max(scores, axis=-1, keepdims=True)
    logsum = highest + jnp.log(jnp.sum(jnp.exp(scores - highest), axis=-1, keepdims=True))
    probs = jnp.exp(scores - logsum).astype(jnp.bfloat16)
    mixed = jnp.einsum("bmhlk,bkmhe->blmhe", probs, values, preferred_element_type=jnp.float32)
    return (mixed.reshape(packed.shape[:-1] + (width,)).astype(jnp.bfloat16), logsum)


def attend_backward(packed, logsum, grad_mixed):
    width = packed.shape[-1] // 3
    query, keys, values = split_heads(packed, width)
    factor = HEAD_DIM ** (-0.5)
    scores = (
        jnp.einsum("blmhe,bkmhe->bmhlk", query, keys, preferred_element_type=jnp.float32) * factor
    )
    probs = jnp.exp(scores - logsum)
    grad_heads = grad_mixed.reshape(query.shape)
    grad_probs = jnp.einsum(
        "blmhe,bkmhe->bmhlk", grad_heads, values, preferred_element_type=jnp.float32
    )
    grad_values = jnp.einsum(
        "bmhlk,blmhe->bkmhe",
        probs.astype(jnp.bfloat16),
        grad_heads,
        preferred_element_type=jnp.float32,
    )
    grad_scores = (
        probs * (grad_probs - jnp.sum(probs * grad_probs, axis=-1, keepdims=True))
    ).astype(jnp.bfloat16)
    grad_query = (
        jnp.einsum("bmhlk,bkmhe->blmhe", grad_scores, keys, preferred_element_type=jnp.float32)
        * factor
    )
    grad_keys = (
        jnp.einsum("bmhlk,blmhe->bkmhe", grad_scores, query, preferred_element_type=jnp.float32)
        * factor
    )
    shape = packed.shape[:-1] + (width,)
    joined = jnp.concatenate(
        [grad_query.reshape(shape), grad_keys.reshape(shape), grad_values.reshape(shape)], axis=-1
    )
    return joined.astype(jnp.bfloat16)


def mixer_forward(resid, shift, scale, gate, qkv_weight, out_weight):
    normed, inverse = layer_norm(resid)
    entry = (normed * (1.0 + scale) + shift).astype(jnp.bfloat16)
    packed = jnp.einsum(
        "blmd,de->blme", entry, qkv_weight, preferred_element_type=jnp.float32
    ).astype(jnp.bfloat16)
    mixed, logsum = attend_forward(packed)
    branch = jnp.einsum("blmd,de->blme", mixed, out_weight, preferred_element_type=jnp.float32)
    return (resid + gate * branch, (normed, inverse, entry, packed, logsum, mixed, branch))


def mixer_backward(grad_out, scale, gate, qkv_weight, out_weight, kept, per_clip):
    normed, inverse, entry, packed, logsum, mixed, branch = kept
    grad_gate = per_clip(grad_out * branch)
    grad_branch = (gate * grad_out).astype(jnp.bfloat16)
    grad_outw = jnp.einsum("blmd,blme->de", mixed, grad_branch, preferred_element_type=jnp.float32)
    grad_mixed = jnp.einsum(
        "blme,de->blmd", grad_branch, out_weight, preferred_element_type=jnp.float32
    ).astype(jnp.bfloat16)
    grad_packed = attend_backward(packed, logsum, grad_mixed)
    grad_qkvw = jnp.einsum("blmd,blme->de", entry, grad_packed, preferred_element_type=jnp.float32)
    grad_entry = jnp.einsum(
        "blme,de->blmd", grad_packed, qkv_weight, preferred_element_type=jnp.float32
    )
    grad_shift = per_clip(grad_entry)
    grad_scale = per_clip(grad_entry * normed)
    grad_in = grad_out + norm_back(grad_entry * (1.0 + scale), normed, inverse)
    return (grad_in, (grad_shift, grad_scale, grad_gate), grad_qkvw, grad_outw)


def feed_forward(resid, shift, scale, gate, up_full, up_bias_full, down_full, down_bias_full):
    normed, inverse = layer_norm(resid)
    entry = (normed * (1.0 + scale) + shift).astype(jnp.bfloat16)
    upward = jnp.einsum(
        "blmd,df->blmf", entry, up_full, preferred_element_type=jnp.float32
    ) + up_bias_full.astype(jnp.float32)
    active = jax.nn.gelu(upward, approximate=False).astype(jnp.bfloat16)
    downward = jnp.einsum(
        "blmf,fd->blmd", active, down_full, preferred_element_type=jnp.float32
    ) + down_bias_full.astype(jnp.float32)
    return (resid + gate * downward, (normed, inverse, entry, upward, active, downward))


def feed_backward(grad_out, scale, gate, up_full, down_full, kept, per_clip):
    normed, inverse, entry, upward, active, downward = kept
    grad_gate = per_clip(grad_out * downward)
    grad_down_in = (gate * grad_out).astype(jnp.bfloat16)
    grad_down = jnp.einsum(
        "blmf,blmd->fd", active, grad_down_in, preferred_element_type=jnp.float32
    )
    grad_down_bias = jnp.sum(grad_down_in.astype(jnp.float32), axis=(0, 1, 2))
    grad_active = jnp.einsum(
        "blmd,fd->blmf", grad_down_in, down_full, preferred_element_type=jnp.float32
    )
    _, gelu_back = jax.vjp(partial(jax.nn.gelu, approximate=False), upward)
    grad_up_in = gelu_back(grad_active)[0].astype(jnp.bfloat16)
    grad_up = jnp.einsum("blmd,blmf->df", entry, grad_up_in, preferred_element_type=jnp.float32)
    grad_up_bias = jnp.sum(grad_up_in.astype(jnp.float32), axis=(0, 1, 2))
    grad_entry = jnp.einsum(
        "blmf,df->blmd", grad_up_in, up_full, preferred_element_type=jnp.float32
    )
    grad_shift = per_clip(grad_entry)
    grad_scale = per_clip(grad_entry * normed)
    grad_in = grad_out + norm_back(grad_entry * (1.0 + scale), normed, inverse)
    return (
        grad_in,
        (grad_shift, grad_scale, grad_gate),
        grad_up,
        grad_up_bias,
        grad_down,
        grad_down_bias,
    )


def body(
    frames_in,
    cotangent,
    time_table,
    ada_weight,
    ada_bias,
    space_qkv,
    space_out,
    time_qkv,
    time_out,
    up_weight,
    up_bias,
    down_weight,
    down_bias,
    timesteps,
    task_mask,
    clip_weight,
    frame_table,
):
    shards = lax.axis_size("shard")
    shard_at = lax.axis_index("shard")
    frame_count, patches, width = frames_in.shape
    clips = timesteps.shape[0]
    frames = task_mask.shape[1]
    table = frame_table[0]
    group_frames = table.shape[0]
    columns = patches // shards
    space_qkv_full = lax.all_gather(space_qkv, "shard", axis=0, tiled=True)
    space_out_full = lax.all_gather(space_out, "shard", axis=0, tiled=True)
    time_qkv_full = lax.all_gather(time_qkv, "shard", axis=0, tiled=True)
    time_out_full = lax.all_gather(time_out, "shard", axis=0, tiled=True)
    up_full = lax.all_gather(up_weight, "shard", axis=0, tiled=True)
    down_full = lax.all_gather(down_weight, "shard", axis=0, tiled=True)
    embed = jnp.take(time_table, timesteps, axis=0).astype(jnp.float32)
    cond = jax.nn.silu(embed).astype(jnp.bfloat16)
    mod_local = jnp.dot(cond, ada_weight, preferred_element_type=jnp.float32)

    def spread(local):
        full = jnp.zeros((shards, local.shape[0]), jnp.float32)
        return lax.dynamic_update_slice_in_dim(
            full, local.astype(jnp.float32)[None], shard_at, 0
        ).reshape(-1)

    small = jnp.concatenate(
        [(mod_local + spread(ada_bias)[None]).reshape(-1), spread(up_bias), spread(down_bias)]
    )
    small = lax.psum(small, "shard")
    modul = small[: clips * 9 * width].reshape(clips, 9 * width)
    up_bias_full = small[clips * 9 * width : -width]
    down_bias_full = small[-width:]
    slot_ids = shard_at * frame_count + jnp.arange(frame_count, dtype=jnp.int32)
    frame_ids = jnp.take(table, slot_ids)
    clip_of = frame_ids // frames
    frame_of = frame_ids % frames
    clip_hot = (clip_of[:, None] == jnp.arange(clips, dtype=jnp.int32)[None, :]).astype(jnp.float32)
    frame_mod = jnp.take(modul, clip_of, axis=0)
    own_parts = [
        frame_mod[:, part_at * width : (part_at + 1) * width][:, None, None, :]
        for part_at in range(9)
    ]
    all_parts = [
        modul[:, part_at * width : (part_at + 1) * width][:, None, None, :] for part_at in range(9)
    ]
    inverse = (
        jnp.zeros((group_frames,), jnp.int32)
        .at[table]
        .set(jnp.arange(group_frames, dtype=jnp.int32))
    )

    def frame_sums(values):
        return jnp.dot(clip_hot.T, jnp.sum(values, axis=(1, 2)), precision=HIGH)

    def column_sums(values):
        return jnp.sum(values, axis=(1, 2))

    def to_columns(rows):
        parts = rows.astype(jnp.bfloat16).reshape(frame_count, shards, columns, width)
        parts = jnp.swapaxes(parts, 0, 1)
        moved = lax.all_to_all(parts, "shard", split_axis=0, concat_axis=0, tiled=True)
        return moved.reshape(group_frames, columns, width)

    def to_frames(cols):
        parts = cols.astype(jnp.bfloat16).reshape(shards, frame_count, columns, width)
        moved = lax.all_to_all(parts, "shard", split_axis=0, concat_axis=0, tiled=True)
        moved = jnp.swapaxes(moved, 0, 1)
        return moved.reshape(frame_count, patches, width).astype(jnp.float32)

    space_rows = frames_in.reshape(frame_count, patches, 1, width)
    after_space, space_kept = mixer_forward(
        space_rows, own_parts[0], own_parts[1], own_parts[2], space_qkv_full, space_out_full
    )
    received = to_columns(after_space.reshape(frame_count, patches, width))
    columned = jnp.take(received, inverse, axis=0).reshape(clips, frames, columns, width)
    columned = columned.astype(jnp.float32)
    after_time, time_kept = mixer_forward(
        columned, all_parts[3], all_parts[4], all_parts[5], time_qkv_full, time_out_full
    )
    result, mlp_kept = feed_forward(
        after_time,
        all_parts[6],
        all_parts[7],
        all_parts[8],
        up_full,
        up_bias_full,
        down_full,
        down_bias_full,
    )
    leaving = jnp.take(result.reshape(group_frames, columns, width), table, axis=0)
    frames_out = to_frames(leaving)
    row_weights = task_mask[clip_of, frame_of].astype(jnp.float32) * clip_weight[clip_of]
    weighted = cotangent * row_weights[:, None, None]
    arriving = to_columns(weighted)
    grad_result = jnp.take(arriving, inverse, axis=0).reshape(clips, frames, columns, width)
    grad_result = grad_result.astype(jnp.float32)
    grad_after_time, mlp_mods, grad_up, grad_up_bias, grad_down, grad_down_bias = feed_backward(
        grad_result, all_parts[7], all_parts[8], up_full, down_full, mlp_kept, column_sums
    )
    grad_columned, time_mods, grad_time_qkv, grad_time_out = mixer_backward(
        grad_after_time,
        all_parts[4],
        all_parts[5],
        time_qkv_full,
        time_out_full,
        time_kept,
        column_sums,
    )
    going = jnp.take(grad_columned.reshape(group_frames, columns, width), table, axis=0)
    grad_space = to_frames(going)
    grad_rows, space_mods, grad_space_qkv, grad_space_out = mixer_backward(
        grad_space.reshape(frame_count, patches, 1, width),
        own_parts[1],
        own_parts[2],
        space_qkv_full,
        space_out_full,
        space_kept,
        frame_sums,
    )
    mod_part = jnp.concatenate(space_mods + time_mods + mlp_mods, axis=1)
    small_grads = jnp.concatenate([mod_part.reshape(-1), grad_up_bias, grad_down_bias])
    small_grads = lax.psum(small_grads, "shard")
    mod_size = clips * 9 * width
    grad_modul = small_grads[:mod_size].reshape(clips, 9 * width).astype(jnp.bfloat16)
    up_dev = up_bias.shape[0]
    down_dev = down_bias.shape[0]
    bias_dev = ada_bias.shape[0]
    every_modul = lax.all_gather(grad_modul, "grp", axis=0, tiled=True)
    bias_sums = lax.psum(
        jnp.concatenate(
            [
                lax.dynamic_slice_in_dim(small_grads, mod_size + shard_at * up_dev, up_dev, 0),
                lax.dynamic_slice_in_dim(
                    small_grads, mod_size + shards * up_dev + shard_at * down_dev, down_dev, 0
                ),
            ]
        ),
        "grp",
    )
    every_embed = lax.all_gather(embed.astype(jnp.bfloat16), "grp", axis=0, tiled=True)
    every_embed = every_embed.astype(jnp.float32)
    groups = lax.axis_size("grp")
    step_slots = jnp.zeros((groups, clips), jnp.float32)
    step_slots = lax.dynamic_update_slice_in_dim(
        step_slots, timesteps.astype(jnp.float32)[None], lax.axis_index("grp"), 0
    )
    every_steps = lax.psum(step_slots.reshape(-1), "grp").astype(jnp.int32)
    every_cond = jax.nn.silu(every_embed).astype(jnp.bfloat16)
    grad_ada = jnp.einsum("cd,cj->dj", every_cond, every_modul, preferred_element_type=jnp.float32)
    grad_ada_bias = lax.dynamic_slice_in_dim(
        jnp.sum(every_modul.astype(jnp.float32), axis=0), shard_at * bias_dev, bias_dev, 0
    )
    grad_cond = jnp.einsum("cj,dj->cd", every_modul, ada_weight, preferred_element_type=jnp.float32)
    _, silu_back = jax.vjp(jax.nn.silu, every_embed)
    grad_embed = silu_back(grad_cond)[0]
    vocab = time_table.shape[0]
    onehot = (jnp.arange(vocab, dtype=jnp.int32)[:, None] == every_steps[None, :]).astype(
        jnp.float32
    )
    grad_table = jnp.dot(onehot, grad_embed, precision=HIGH)

    def total(parts):
        flat = [part.astype(jnp.bfloat16).reshape(shards, -1, width) for part in parts]
        rows = [part.shape[1] for part in flat]
        packed = jnp.concatenate(flat, axis=1)
        share = lax.psum_scatter(packed, "shard", scatter_dimension=0, tiled=True)[0]
        share = lax.psum(share, "grp").astype(jnp.float32)
        out, at = ([], 0)
        for part, count in zip(parts, rows):
            piece = share[at : at + count].reshape(part.shape[0] // shards, part.shape[1])
            out.append(piece)
            at += count
        return out

    grad_up, grad_down = total([grad_up, grad_down])
    grad_time_qkv, grad_time_out = total([grad_time_qkv, grad_time_out])
    grad_space_qkv, grad_space_out = total([grad_space_qkv, grad_space_out])
    return (
        frames_out,
        grad_rows.reshape(frame_count, patches, width),
        grad_table,
        grad_ada,
        grad_ada_bias,
        grad_space_qkv,
        grad_space_out,
        grad_time_qkv,
        grad_time_out,
        grad_up,
        bias_sums[:up_dev],
        grad_down,
        bias_sums[up_dev:],
    )


def solution(mesh):
    placed = (
        P(("grp", "shard"), None, None),
        P(("grp", "shard"), None, None),
        P(None, "shard"),
        P("shard", None),
        P("shard"),
        P("shard", None),
        P("shard", None),
        P("shard", None),
        P("shard", None),
        P("shard", None),
        P("shard"),
        P("shard", None),
        P("shard"),
        P("grp"),
        P("grp", None),
        P("grp"),
        P("grp", None),
    )
    return jax.shard_map(
        body,
        mesh=mesh,
        in_specs=placed,
        out_specs=(
            P(("grp", "shard"), None, None),
            P(("grp", "shard"), None, None),
            P(None, "shard"),
            P("shard", None),
            P("shard"),
            P("shard", None),
            P("shard", None),
            P("shard", None),
            P("shard", None),
            P("shard", None),
            P("shard"),
            P("shard", None),
            P("shard"),
        ),
        check_vma=False,
    )
```

profile of v0, /device:TPU:0, one launch (start us, length us, event | category | flops | bytes accessed | tf_op | source)
XLA Modules:
  0.0 886.2 jit_solution(1337077079453278443)
XLA Ops:
  34.7 35.1 %all-reduce.6.cloned.1.call-done = f32[17664]{0:T(1024)} async-done(((f32[17664]{0:T(1024)}), f32[17664]{0:T(1024)}) %all-reduce.6.cloned.1.call-update) | async-done | bytes 70672 | tf_op jit(solution)/shard_map/psum | solution.py:204
  71.3 35.3 %all-gather.9.cloned.1.call-done = bf16[768,2304]{1,0:T(8,128)(2,1)} async-done(((bf16[96,2304]{1,0:T(8,128)(2,1)}), bf16[768,2304]{1,0:T(8,128)(2,1)}) %all-gather.9.cloned.1.call-update) | async-done | bytes 3538960 | tf_op jit(solution)/shard_map/all_gather | solution.py:185
  106.7 7.0 fusion.9
  129.4 8.7 convolution_convert_fusion.3
  156.2 23.0 %all-to-all-done = bf16[8,4,32,768]{3,2,1,0:T(8,128)(2,1)S(1)} async-done(((bf16[8,4,32,768]{3,2,1,0:T(8,128)(2,1)}), bf16[8,4,32,768]{3,2,1,0:T(8,128)(2,1)S(1)}, u32[]{:S(2)}, u32[]{:S(2)}) %all-to-all-start) | async-done | bytes 1572896 | tf_op jit(solution)/shard_map/all_to_all | solution.py:236
  189.8 7.0 convolution_convert_fusion
  217.0 8.0 multiply_reduce_fusion.3
  255.4 11.7 %fusion.8 = (u16[2,32,3072]{2,1,0:T(8,128)(2,1)S(1)}, u16[2,32,3072]{2,1,0:T(8,128)(2,1)S(1)}, f32[2,16,32,3072]{3,2,1,0:T(8,128)S(1)}) fusion(f32[3072]{0:T(1024)S(1)} %slice.149, bf16[768,3072]{1,0:T(8,128)(2,1)} %all-gather.17.cloned.1.call-done, f32[2,16,32,768]{3,2,1,0:T(8,128)} %get-tuple-element.73, f32[2,768]{1,0:T(2,128)S(1)} %get-tuple-element.54, ...), kind=kOutput, calls=%fused_computation.51 | convolution fusion | flops 4879417344 | bytes 21266432 | tf_op jit(solution)/shard_map/blmd,df->blmf/dot_general | solution.py:117
  272.0 29.8 %multiply_convert_fusion.1 = (bf16[2,16,32,3072]{3,2,1,0:T(8,128)(2,1)}, f32[2,16,32,3072]{3,2,1,0:T(8,128)}) fusion(f32[2,16,32,3072]{3,2,1,0:T(8,128)S(1)} %get-tuple-element.75, f32[3072]{0:T(1024)S(1)} %slice.149, u16[2,32,3072]{2,1,0:T(8,128)(2,1)S(1)} %get-tuple-element.16, u16[2,32,3072]{2,1,0:T(8,128)(2,1)S(1)} %get-tuple-element.15), kind=kLoop, calls=%fused_computation.21 | loop fusion | flops 223346688 | bytes 32256000 | tf_op jit(solution)/shard_map/convert_element_type | solution.py:120
  301.7 19.7 %convert_reduce_fusion = (f32[3072]{0:T(1024)}, bf16[2,16,32,3072]{3,2,1,0:T(8,128)(2,1)}) fusion(f32[2,16,32,3072]{3,2,1,0:T(8,128)} %get-tuple-element.37, bf16[3072,768]{1,0:T(8,128)(2,1)} %all-gather.19.cloned.1.call-done, f32[2,16,32,768]{3,2,1,0:T(8,128)} %bitcast.240, f32[2,768]{1,0:T(2,128)S(1)} %get-tuple-element.55, ...), kind=kOutput, calls=%fused_computation.17 | convolution fusion | flops 4886885376 | bytes 39352320 | tf_op jit(solution)/shard_map/blmd,fd->blmf/dot_general | solution.py:135
  321.4 10.0 %multiply_reduce_fusion.5 = (f32[2,768]{1,0:T(2,128)}, f32[2,16,32]{2,1,0:T(8,128)S(1)}, f32[2,16,32]{2,1,0:T(8,128)S(1)}, f32[2,768]{1,0:T(2,128)}, f32[2,16,32,768]{3,2,1,0:T(8,128)S(1)}) fusion(f32[2,16,32,768]{3,2,1,0:T(8,128)S(1)} %copy-done.10, f32[2,16,32]{2,1,0:T(8,128)S(1)} %add_rsqrt_fusion, f32[2,16,32]{2,1,0:T(8,128)S(1)} %broadcast_multiply_fusion.4, ...), kind=kOutput, calls=%fused_computation.88 | convolution fusion | flops 4838910976 | bytes 17336320 | tf_op jit(solution)/shard_map/blmf,df->blmd/dot_general | solution.py:142
  344.2 13.1 %multiply_reduce_fusion.2 = (f32[2,32,12,16]{3,2,1,0:T(8,128)S(1)}, f32[2,32,12,16,16]{3,4,2,1,0:T(8,128)}) fusion(f32[2,32,12,16,16]{3,4,2,1,0:T(8,128)} %copy-done.5, f32[2,32,12,16]{3,2,1,0:T(8,128)} %copy-done.28, bf16[2,16,32,12,64]{4,3,2,1,0:T(8,128)(2,1)} %reshape.638, bf16[2,16,32,12,64]{4,3,2,1,0:T(8,128)(2,1)} %reshape.645), kind=kOutput, calls=%fused_computation.47 | convolution fusion | flops 25939968 | bytes 4816896 | tf_op jit(solution)/shard_map/blmhe,bkmhe->bmhlk/dot_general | solution.py:57
  413.9 6.8 reshape.657
  425.4 10.9 %multiply_reduce_fusion.7 = (f32[2,768]{1,0:T(2,128)}, f32[2,16,32]{2,1,0:T(8,128)S(1)}, f32[2,16,32]{2,1,0:T(8,128)S(1)}, f32[2,768]{1,0:T(2,128)}, f32[2,16,32,768]{3,2,1,0:T(8,128)}) fusion(f32[2,16,32,768]{3,2,1,0:T(8,128)} %bitcast.258, f32[2,16,32]{2,1,0:T(8,128)S(1)} %bitcast.274, f32[2,16,32]{2,1,0:T(8,128)S(1)} %bitcast.270, ...), kind=kOutput, calls=%fused_computation.90 | convolution fusion | flops 3630951424 | bytes 14583808 | tf_op jit(solution)/shard_map/blme,de->blmd/dot_general | solution.py:105
  436.3 9.3 %multiply_add_fusion.2 = (bf16[2,16,32,768]{3,2,1,0:T(8,128)(2,1)}, f32[2,16,32,768]{3,2,1,0:T(8,128)}) fusion(f32[2,16,32,768]{3,2,1,0:T(8,128)S(1)} %copy-done.11, f32[768]{0:T(1024)S(1)} %copy-done.61, f32[2,768]{1,0:T(2,128)S(1)} %get-tuple-element.55, bf16[2,16,32,3072]{3,2,1,0:T(8,128)(2,1)S(1)} %bitcast.250, ...), kind=kOutput, calls=%fused_computation.103 | convolution fusion | flops 4834983936 | bytes 18883584 | tf_op jit(solution)/shard_map/blmf,fd->blmd/dot_general | solution.py:121
  465.0 10.6 %bitcast_convert_fusion.1 = bf16[768,3072]{1,0:T(8,128)(2,1)} fusion(bf16[2,16,32,3072]{3,2,1,0:T(8,128)(2,1)} %get-tuple-element.86, f32[2,16,32,768]{3,2,1,0:T(8,128)} %get-tuple-element.73, f32[2,768]{1,0:T(2,128)S(1)} %copy-done.66, f32[2,768]{1,0:T(2,128)S(1)} %get-tuple-element.53, f32[2,16,32]{2,1,0:T(8,128)S(1)} %add_rsqrt_fusion, ...), kind=kOutput, calls=%fused_computation.39 | convolution fusion | flops 4838129664 | bytes 14176256 | tf_op jit(solution)/shard_map/blmd,blmf->df/dot_general | solution.py:140
  475.6 8.5 reshape.660
  484.1 8.0 all-to-all-done.3
  502.9 8.1 convolution_convert_fusion.2
  513.7 6.9 multiply_reduce_fusion
  520.6 7.6 multiply_convert_fusion
  542.8 8.8 bitcast_convert_fusion.3
  563.9 8.2 bitcast_convert_fusion
  572.1 6.9 pad_maximum_fusion
  591.2 7.0 multiply_reduce_fusion.8
  602.7 29.1 %reduce-scatter.4.cloned.1.call-done = bf16[1,384,768]{2,1,0:T(8,128)(2,1)} async-done(((bf16[8,384,768]{2,1,0:T(8,128)(2,1)}), bf16[1,384,768]{2,1,0:T(8,128)(2,1)}) %reduce-scatter.4.cloned.1.call-update) | async-done | bytes 589840 | tf_op jit(solution)/shard_map/reduce_scatter | solution.py:341
  631.8 80.2 %reduce-scatter.8.cloned.1.call-done = bf16[1,768,768]{2,1,0:T(8,128)(2,1)} async-done(((bf16[8,768,768]{2,1,0:T(8,128)(2,1)}), bf16[1,768,768]{2,1,0:T(8,128)(2,1)}) %reduce-scatter.8.cloned.1.call-update) | async-done | bytes 1179664 | tf_op jit(solution)/shard_map/reduce_scatter | solution.py:341
  712.2 10.9 %all-gather.1 = bf16[4,2,96]{2,1,0:T(2,128)(2,1)S(1)} all-gather(bf16[1,2,96]{2,1,0:T(2,128)(2,1)S(1)} %fusion.91), channel_id=1, replica_groups=mesh['grp'=4,'shard'=8] {'grp'}, dimensions={0}, use_global_device_ids=true | all-gather | bytes 1920 | tf_op jit(solution)/shard_map/all_gather | solution.py:315
  723.1 42.7 %all-reduce.8.cloned.1.call-done = f32[17664]{0:T(1024)} async-done(((f32[17664]{0:T(1024)}), f32[17664]{0:T(1024)}) %all-reduce.8.cloned.1.call-update) | async-done | bytes 70672 | tf_op jit(solution)/shard_map/psum | solution.py:297
  769.4 12.1 %all-reduce = (f32[8]{0:T(128)S(1)}, f32[480]{0:T(512)S(1)}) all-reduce(f32[8]{0:T(128)S(1)} %reshape.652, f32[480]{0:T(512)S(1)} %pad_maximum_fusion.8), channel_id=1, replica_groups=mesh['grp'=4,'shard'=8] {'grp'}, use_global_device_ids=true, to_apply=%region_20.23 | all-reduce | flops 488 | bytes 3904 | tf_op jit(solution)/shard_map/psum | solution.py:322
  782.9 14.5 %all-gather = bf16[4,2,6912]{2,1,0:T(2,128)(2,1)S(1)} all-gather(bf16[1,2,6912]{2,1,0:T(2,128)(2,1)S(1)} %reshape.753), channel_id=1, replica_groups=mesh['grp'=4,'shard'=8] {'grp'}, dimensions={0}, use_global_device_ids=true | all-gather | bytes 138240 | tf_op jit(solution)/shard_map/all_gather | solution.py:303
  801.9 64.0 %all-reduce.10.cloned.1.call-done = (bf16[384,768]{1,0:T(8,128)(2,1)}, bf16[384,768]{1,0:T(8,128)(2,1)}, bf16[768,768]{1,0:T(8,128)(2,1)}) async-done(((bf16[384,768]{1,0:T(8,128)(2,1)}, bf16[384,768]{1,0:T(8,128)(2,1)}, bf16[768,768]{1,0:T(8,128)(2,1)}), (bf16[384,768]{1,0:T(8,128)(2,1)}, bf16[384,768]{1,0:T(8,128)(2,1)}, bf16[768,768]{1,0:T(8,128)(2,1)})) %all-reduce.10.cloned.1.call-update) | async-done | bytes 2359312 | tf_op jit(solution)/shard_map/psum | solution.py:342
  (370 shorter events, 300.9 us)
Async XLA Ops:
  7.2 62.5 %all-reduce.6.cloned.1.call-start = ((), (), s32[]{:S(2)}) async-start(), calls=%async_computation.7 | async-start | bytes 147456 | tf_op jit(solution)/shard_map/psum | solution.py:204
  8.0 15.1 %copy-start.73 = (pred[2]{0:T(512)(128)(4,1)}, pred[2]{0:T(512)(128)(4,1)S(1)}, u32[]{:S(2)}) copy-start(pred[2]{0:T(512)(128)(4,1)S(1)} %compare_and_fusion.2) | copy-start | bytes 10
  15.7 91.0 %all-gather.9.cloned.1.call-start = ((), (), s32[]{:S(2)}) async-start(), calls=%async_computation.8 | async-start | bytes 3981312 | tf_op jit(solution)/shard_map/all_gather | solution.py:185
  16.5 121.6 %all-gather.11.cloned.1.call-start = ((), (), s32[]{:S(2)}) async-start(), calls=%async_computation.9 | async-start | bytes 1327104 | tf_op jit(solution)/shard_map/all_gather | solution.py:186
  17.2 172.6 %all-gather.13.cloned.1.call-start = ((), (), s32[]{:S(2)}) async-start(), calls=%async_computation.10 | async-start | bytes 3981312 | tf_op jit(solution)/shard_map/all_gather | solution.py:187
  17.8 227.1 %all-gather.15.cloned.1.call-start = ((), (), s32[]{:S(2)}) async-start(), calls=%async_computation.11 | async-start | bytes 1327104 | tf_op jit(solution)/shard_map/all_gather | solution.py:188
  18.4 237.0 %all-gather.17.cloned.1.call-start = ((), (), s32[]{:S(2)}) async-start(), calls=%async_computation.12 | async-start | bytes 5308416 | tf_op jit(solution)/shard_map/all_gather | solution.py:189
  24.4 120.8 %all-to-all-start.2 = ((bf16[8,4,32,768]{3,2,1,0:T(8,128)(2,1)}), bf16[8,4,32,768]{3,2,1,0:T(8,128)(2,1)}, u32[]{:S(2)}, u32[]{:S(2)}) async-start(bf16[8,4,32,768]{3,2,1,0:T(8,128)(2,1)} %copy.168), calls=%async_computation.2 | async-start | bytes 3145728 | tf_op jit(solution)/shard_map/all_to_all | solution.py:236
  32.3 81.4 %copy-start.56 = (f32[4,256]{1,0:T(4,128)}, f32[4,256]{1,0:T(4,128)S(1)}, u32[]{:S(2)}) copy-start(f32[4,256]{1,0:T(4,128)S(1)} %broadcast_multiply_fusion.8) | copy-start | bytes 12292
  34.7 79.1 %copy-start.59 = (f32[4,256]{1,0:T(4,128)}, f32[4,256]{1,0:T(4,128)S(1)}, u32[]{:S(2)}) copy-start(f32[4,256]{1,0:T(4,128)S(1)} %add_rsqrt_fusion.2) | copy-start | bytes 12292
  71.3 42.4 %copy-start.54 = (f32[4,768]{1,0:T(4,128)}, f32[4,768]{1,0:T(4,128)S(1)}, u32[]{:S(2)}) copy-start(f32[4,768]{1,0:T(4,128)S(1)} %get-tuple-element.52) | copy-start | bytes 36868
  71.3 42.4 %copy-start.62 = (f32[4,768]{1,0:T(4,128)}, f32[4,768]{1,0:T(4,128)S(1)}, u32[]{:S(2)}) copy-start(f32[4,768]{1,0:T(4,128)S(1)} %get-tuple-element.51) | copy-start | bytes 36868
  71.3 66.7 %copy-start.52 = (f32[4,768]{1,0:T(4,128)}, f32[4,768]{1,0:T(4,128)S(1)}, u32[]{:S(2)}) copy-start(f32[4,768]{1,0:T(4,128)S(1)} %get-tuple-element.50) | copy-start | bytes 36868
  145.2 34.0 %all-to-all-start = ((bf16[8,4,32,768]{3,2,1,0:T(8,128)(2,1)}), bf16[8,4,32,768]{3,2,1,0:T(8,128)(2,1)S(1)}, u32[]{:S(2)}, u32[]{:S(2)}) async-start(bf16[8,4,32,768]{3,2,1,0:T(8,128)(2,1)} %bitcast.226), calls=%async_computation | async-start | bytes 3145728 | tf_op jit(solution)/shard_map/all_to_all | solution.py:236
  148.8 153.0 %all-gather.19.cloned.1.call-start = ((), (), s32[]{:S(2)}) async-start(), calls=%async_computation.13 | async-start | bytes 5308416 | tf_op jit(solution)/shard_map/all_gather | solution.py:190
  149.5 453.2 %reduce-scatter.6.cloned.1.call-start = ((), (), s32[]{:S(2)}) async-start(), calls=%async_computation.16 | async-start | bytes 5308416 | tf_op jit(solution)/shard_map/reduce_scatter | solution.py:341
  152.9 102.4 %copy-start.65 = (f32[2,768]{1,0:T(2,128)}, f32[2,768]{1,0:T(2,128)S(1)}, u32[]{:S(2)}) copy-start(f32[2,768]{1,0:T(2,128)S(1)} %get-tuple-element.54) | copy-start | bytes 18436
  182.4 62.6 %copy-start.6 = (bf16[32,32,768]{2,1,0:T(8,128)(2,1)}, bf16[32,32,768]{2,1,0:T(8,128)(2,1)S(1)}, u32[]{:S(2)}) copy-start(bf16[32,32,768]{2,1,0:T(8,128)(2,1)S(1)} %gather_fusion.5) | copy-start | bytes 4718596
  301.7 19.7 %copy-start.10 = (f32[2,16,32,768]{3,2,1,0:T(8,128)S(1)}, f32[2,16,32,768]{3,2,1,0:T(8,128)}, u32[]{:S(2)}) copy-start(f32[2,16,32,768]{3,2,1,0:T(8,128)} %get-tuple-element.73) | copy-start | bytes 9437188
  338.0 19.4 %slice-start = ((s8[6291456]{0:T(1024)(128)(4,1)}), s8[2097152]{0:T(1024)(128)(4,1)S(1)}, s32[]{:S(2)}) async-start(s8[6291456]{0:T(1024)(128)(4,1)} %bitcast.230), calls=%async_computation.19 | async-start | bytes 4194304
  344.2 13.1 %slice-start.1 = ((s8[6291456]{0:T(1024)(128)(4,1)}), s8[4194304]{0:T(1024)(128)(4,1)S(1)}, s32[]{:S(2)}) async-start(s8[6291456]{0:T(1024)(128)(4,1)} %bitcast.230), calls=%async_computation.20 | async-start | bytes 8388608
  461.2 30.9 %all-to-all-start.3 = ((bf16[8,4,32,768]{3,2,1,0:T(8,128)(2,1)}), bf16[8,4,32,768]{3,2,1,0:T(8,128)(2,1)S(1)}, u32[]{:S(2)}, u32[]{:S(2)}) async-start(bf16[8,4,32,768]{3,2,1,0:T(8,128)(2,1)} %bitcast.248), calls=%async_computation.3 | async-start | bytes 3145728 | tf_op jit(solution)/shard_map/all_to_all | solution.py:241
  465.0 166.9 %reduce-scatter.4.cloned.1.call-start = ((), (), s32[]{:S(2)}) async-start(), calls=%async_computation.15 | async-start | bytes 5308416 | tf_op jit(solution)/shard_map/reduce_scatter | solution.py:341
  475.6 16.5 %copy-start.53 = (f32[4,768]{1,0:T(4,128)S(1)}, f32[4,768]{1,0:T(4,128)}, u32[]{:S(2)}) copy-start(f32[4,768]{1,0:T(4,128)} %copy-done.52) | copy-start | bytes 36868
  563.9 148.1 %reduce-scatter.8.cloned.1.call-start = ((), (), s32[]{:S(2)}) async-start(), calls=%async_computation.17 | async-start | bytes 10616832 | tf_op jit(solution)/shard_map/reduce_scatter | solution.py:341
  579.1 188.3 %all-to-all-start.1 = ((bf16[8,4,32,768]{3,2,1,0:T(8,128)(2,1)}), bf16[8,4,32,768]{3,2,1,0:T(8,128)(2,1)S(1)}, u32[]{:S(2)}, u32[]{:S(2)}) async-start(bf16[8,4,32,768]{3,2,1,0:T(8,128)(2,1)} %bitcast.32), calls=%async_computation.1 | async-start | bytes 3145728 | tf_op jit(solution)/shard_map/all_to_all | solution.py:241
  582.7 183.1 %all-reduce.8.cloned.1.call-start = ((), (), s32[]{:S(2)}) async-start(), calls=%async_computation.14 | async-start | bytes 147456 | tf_op jit(solution)/shard_map/psum | solution.py:297
  598.9 113.1 %copy-start.76 = (f32[1,2]{1,0:T(1,128)S(1)}, f32[1,2]{1,0:T(1,128)}, u32[]{:S(2)}) copy-start(f32[1,2]{1,0:T(1,128)} %get-tuple-element.59) | copy-start | bytes 28
  598.9 113.2 %copy-start.72 = (bf16[2,96]{1,0:T(2,128)(2,1)S(1)}, bf16[2,96]{1,0:T(2,128)(2,1)}, u32[]{:S(2)}) copy-start(bf16[2,96]{1,0:T(2,128)(2,1)} %copy-done.71) | copy-start | bytes 1156
  598.9 113.2 %copy-start.74 = (pred[2]{0:T(512)(128)(4,1)S(1)}, pred[2]{0:T(512)(128)(4,1)}, u32[]{:S(2)}) copy-start(pred[2]{0:T(512)(128)(4,1)} %copy-done.73) | copy-start | bytes 10
  602.7 263.3 %all-reduce.10.cloned.1.call-start = ((), (), s32[]{:S(2)}) async-start(), calls=%async_computation.18 | async-start | bytes 4718592 | tf_op jit(solution)/shard_map/psum | solution.py:342
  781.5 87.3 %copy-start.78 = (f32[480]{0:T(512)}, f32[480]{0:T(512)S(1)}, u32[]{:S(2)}) copy-start(f32[480]{0:T(512)S(1)} %get-tuple-element.32) | copy-start | bytes 5764
  (67 other events, 334.5 us)
Sparse Core Ops, SparseCore 0:
  15.8 53.8 all-reduce.5
  71.6 35.0 all-gather.8
  108.6 23.9 all-gather.10
  134.3 43.2 all-gather.12
  179.3 26.1 all-gather.14
  207.3 38.7 all-gather.16
  248.0 38.7 all-gather.18
  425.4 62.8 reduce-scatter.5
  564.0 67.7 reduce-scatter.3
  635.2 76.7 reduce-scatter.7
  715.6 50.1 all-reduce.7
  768.2 97.7 all-reduce.9
where the time goes:
time: 898 us; the launch traced here: 886 us
  waiting for transfers between devices  321 us (36%)
  matrix products  218 us (24%)
  local copies, waits for them, and re-layouts  173 us (19%)
  other arithmetic  103 us (11%)
  blocking collectives  37.5 us (4%)
  starting transfers between devices  16.7 us (2%)
  between operations  15.7 us (2%)
    reduce_scatter x3, waiting for transfers between devices, total(): lax.psum_scatter(packed, 'shard', scatter_dimension=0, tiled=True)[0]  109 us
    psum x1, waiting for transfers between devices, total(): share = lax.psum(share, 'grp').astype(jnp.float32)  64 us
    psum x1, waiting for transfers between devices, body(): small_grads = lax.psum(small_grads, 'shard')  42.7 us
    all_gather x1, waiting for transfers between devices, body(): space_qkv_full = lax.all_gather(space_qkv, 'shard', axis=0, tiled=True)  35.3 us
    psum x1, waiting for transfers between devices, body(): small = lax.psum(small, 'shard')  35.1 us
    convert_element_type x1, other arithmetic, feed_forward(): active = jax.nn.gelu(upward, approximate=False).astype(jnp.bfloat16)  29.8 us
    unnamed x176, local copies, waits for them, and re-layouts  23.9 us
    all_to_all x2, waiting for transfers between devices, to_columns(): lax.all_to_all(parts, 'shard', split_axis=0, concat_axis=0, tiled=True)  23 us
  transfers between devices with their start and end apart: 16, of which 8 were waited for; matrix products, arithmetic and copies ran while one was open for 37% of the time, Pallas kernels for 0%

commit v1 on v0

--- a/solution.py
+++ b/solution.py
@@ -294,7 +294,7 @@
     )
     mod_part = jnp.concatenate(space_mods + time_mods + mlp_mods, axis=1)
     small_grads = jnp.concatenate([mod_part.reshape(-1), grad_up_bias, grad_down_bias])
-    small_grads = lax.psum(small_grads, "shard")
+    small_grads = jnp.sum(lax.all_gather(small_grads, "shard"), axis=0)
     mod_size = clips * 9 * width
     grad_modul = small_grads[:mod_size].reshape(clips, 9 * width).astype(jnp.bfloat16)
     up_dev = up_bias.shape[0]

time: 898 us -> 843 us (0.939)
  waiting for transfers between devices: 321 us -> 259 us
  blocking collectives: 37.5 us -> 47.6 us
    psum x1 -> x0, waiting for transfers between devices: 42.7 us -> none  [body(): small_grads = lax.psum(small_grads, 'shard')]
    reduce_scatter x3, waiting for transfers between devices: 109 us -> 99 us  [total(): lax.psum_scatter(packed, 'shard', scatter_dimension=0, tiled=True)[0]]
    all_gather x0 -> x1, blocking collectives: none -> 9.93 us  [body(): small_grads = jnp.sum(lax.all_gather(small_grads, 'shard'), axis=0)]
    psum x1, waiting for transfers between devices: 64 us -> 54.6 us  [total(): share = lax.psum(share, 'grp').astype(jnp.float32)]
    unnamed x176 -> x177, local copies, waits for them, and re-layouts: 23.9 us -> 24 us
  transfers between devices with their start and end apart: 16 -> 15, of which waited for: 8 -> 7; matrix products, arithmetic and copies ran while one was open for 37% -> 40% of each run, Pallas kernels for 0% -> 0%
where the time goes in v1:
time: 843 us; the launch traced here: 831 us
  waiting for transfers between devices  259 us (31%)
  matrix products  218 us (26%)
  local copies, waits for them, and re-layouts  171 us (20%)
  other arithmetic  103 us (12%)
  blocking collectives  47.6 us (6%)
  starting transfers between devices  16.7 us (2%)
  between operations  15.4 us (2%)
    reduce_scatter x3, waiting for transfers between devices, total(): lax.psum_scatter(packed, 'shard', scatter_dimension=0, tiled=True)[0]  99 us
    psum x1, waiting for transfers between devices, total(): share = lax.psum(share, 'grp').astype(jnp.float32)  54.6 us
    all_gather x1, waiting for transfers between devices, body(): space_qkv_full = lax.all_gather(space_qkv, 'shard', axis=0, tiled=True)  35.3 us
    psum x1, waiting for transfers between devices, body(): small = lax.psum(small, 'shard')  35 us
    convert_element_type x1, other arithmetic, feed_forward(): active = jax.nn.gelu(upward, approximate=False).astype(jnp.bfloat16)  29.8 us
    unnamed x177, local copies, waits for them, and re-layouts  24 us
    all_to_all x2, waiting for transfers between devices, to_columns(): lax.all_to_all(parts, 'shard', split_axis=0, concat_axis=0, tiled=True)  23 us
    reshape x3, local copies, waits for them, and re-layouts, total(): part.astype(jnp.bfloat16).reshape(shards, -1, width)  22 us
  transfers between devices with their start and end apart: 15, of which 7 were waited for; matrix products, arithmetic and copies ran while one was open for 40% of the time, Pallas kernels for 0%

profile of v1, /device:TPU:0, one launch (start us, length us, event | category | flops | bytes accessed | tf_op | source)
XLA Modules:
  0.0 831.3 jit_solution(50736343671714944)
XLA Ops:
  34.7 35.0 %all-reduce.5.cloned.1.call-done = f32[17664]{0:T(1024)} async-done(((f32[17664]{0:T(1024)}), f32[17664]{0:T(1024)}) %all-reduce.5.cloned.1.call-update) | async-done | bytes 70672 | tf_op jit(solution)/shard_map/psum | solution.py:204
  71.3 35.3 %all-gather.11.cloned.1.call-done = bf16[768,2304]{1,0:T(8,128)(2,1)} async-done(((bf16[96,2304]{1,0:T(8,128)(2,1)}), bf16[768,2304]{1,0:T(8,128)(2,1)}) %all-gather.11.cloned.1.call-update) | async-done | bytes 3538960 | tf_op jit(solution)/shard_map/all_gather | solution.py:185
  106.7 7.0 fusion.9
  129.4 8.7 %convolution_convert_fusion.3 = bf16[4,12,64,256]{3,2,1,0:T(8,128)(2,1)} fusion(bf16[4,256,12,64]{1,3,2,0:T(8,128)(2,1)S(1)} %bitcast.236, f32[4,12,256,256]{2,3,1,0:T(8,128)} %copy-done.3, f32[4,12,256]{2,1,0:T(8,128)S(1)} %log_add_fusion.1), kind=kOutput, calls=%fused_computation.132 | convolution fusion | flops 412876800 | bytes 15777792 | tf_op jit(solution)/shard_map/bmhlk,bkmhe->blmhe/dot_general | solution.py:44
  156.2 23.0 %all-to-all-done = bf16[8,4,32,768]{3,2,1,0:T(8,128)(2,1)S(1)} async-done(((bf16[8,4,32,768]{3,2,1,0:T(8,128)(2,1)}), bf16[8,4,32,768]{3,2,1,0:T(8,128)(2,1)S(1)}, u32[]{:S(2)}, u32[]{:S(2)}) %all-to-all-start) | async-done | bytes 1572896 | tf_op jit(solution)/shard_map/all_to_all | solution.py:236
  189.8 7.0 convolution_convert_fusion
  217.1 8.0 multiply_reduce_fusion.3
  255.4 11.6 %fusion.8 = (u16[2,32,3072]{2,1,0:T(8,128)(2,1)S(1)}, u16[2,32,3072]{2,1,0:T(8,128)(2,1)S(1)}, f32[2,16,32,3072]{3,2,1,0:T(8,128)S(1)}) fusion(f32[3072]{0:T(1024)S(1)} %slice.149, bf16[768,3072]{1,0:T(8,128)(2,1)} %all-gather.19.cloned.1.call-done, f32[2,16,32,768]{3,2,1,0:T(8,128)} %get-tuple-element.73, f32[2,768]{1,0:T(2,128)S(1)} %get-tuple-element.54, ...), kind=kOutput, calls=%fused_computation.51 | convolution fusion | flops 4879417344 | bytes 21266432 | tf_op jit(solution)/shard_map/blmd,df->blmf/dot_general | solution.py:117
  271.9 29.8 %multiply_convert_fusion.1 = (bf16[2,16,32,3072]{3,2,1,0:T(8,128)(2,1)}, f32[2,16,32,3072]{3,2,1,0:T(8,128)}) fusion(f32[2,16,32,3072]{3,2,1,0:T(8,128)S(1)} %get-tuple-element.75, f32[3072]{0:T(1024)S(1)} %slice.149, u16[2,32,3072]{2,1,0:T(8,128)(2,1)S(1)} %get-tuple-element.16, u16[2,32,3072]{2,1,0:T(8,128)(2,1)S(1)} %get-tuple-element.15), kind=kLoop, calls=%fused_computation.21 | loop fusion | flops 223346688 | bytes 32256000 | tf_op jit(solution)/shard_map/convert_element_type | solution.py:120
  301.8 19.7 %convert_reduce_fusion = (f32[3072]{0:T(1024)}, bf16[2,16,32,3072]{3,2,1,0:T(8,128)(2,1)}) fusion(f32[2,16,32,3072]{3,2,1,0:T(8,128)} %get-tuple-element.37, bf16[3072,768]{1,0:T(8,128)(2,1)} %all-gather.21.cloned.1.call-done, f32[2,16,32,768]{3,2,1,0:T(8,128)} %bitcast.240, f32[2,768]{1,0:T(2,128)S(1)} %get-tuple-element.55, ...), kind=kOutput, calls=%fused_computation.17 | convolution fusion | flops 4886885376 | bytes 39352320 | tf_op jit(solution)/shard_map/blmd,fd->blmf/dot_general | solution.py:135
  321.4 10.0 %multiply_reduce_fusion.5 = (f32[2,768]{1,0:T(2,128)}, f32[2,16,32]{2,1,0:T(8,128)S(1)}, f32[2,16,32]{2,1,0:T(8,128)S(1)}, f32[2,768]{1,0:T(2,128)}, f32[2,16,32,768]{3,2,1,0:T(8,128)S(1)}) fusion(f32[2,16,32,768]{3,2,1,0:T(8,128)S(1)} %copy-done.10, f32[2,16,32]{2,1,0:T(8,128)S(1)} %add_rsqrt_fusion, f32[2,16,32]{2,1,0:T(8,128)S(1)} %broadcast_multiply_fusion.4, ...), kind=kOutput, calls=%fused_computation.88 | convolution fusion | flops 4838910976 | bytes 17336320 | tf_op jit(solution)/shard_map/blmf,df->blmd/dot_general | solution.py:142
  344.2 13.1 %multiply_reduce_fusion.2 = (f32[2,32,12,16]{3,2,1,0:T(8,128)S(1)}, f32[2,32,12,16,16]{3,4,2,1,0:T(8,128)}) fusion(f32[2,32,12,16,16]{3,4,2,1,0:T(8,128)} %copy-done.5, f32[2,32,12,16]{3,2,1,0:T(8,128)} %copy-done.28, bf16[2,16,32,12,64]{4,3,2,1,0:T(8,128)(2,1)} %reshape.638, bf16[2,16,32,12,64]{4,3,2,1,0:T(8,128)(2,1)} %reshape.645), kind=kOutput, calls=%fused_computation.47 | convolution fusion | flops 25939968 | bytes 4816896 | tf_op jit(solution)/shard_map/blmhe,bkmhe->bmhlk/dot_general | solution.py:57
  414.0 6.8 reshape.657
  425.4 10.9 %multiply_reduce_fusion.7 = (f32[2,768]{1,0:T(2,128)}, f32[2,16,32]{2,1,0:T(8,128)S(1)}, f32[2,16,32]{2,1,0:T(8,128)S(1)}, f32[2,768]{1,0:T(2,128)}, f32[2,16,32,768]{3,2,1,0:T(8,128)}) fusion(f32[2,16,32,768]{3,2,1,0:T(8,128)} %bitcast.258, f32[2,16,32]{2,1,0:T(8,128)S(1)} %bitcast.274, f32[2,16,32]{2,1,0:T(8,128)S(1)} %bitcast.270, ...), kind=kOutput, calls=%fused_computation.90 | convolution fusion | flops 3630951424 | bytes 14583808 | tf_op jit(solution)/shard_map/blme,de->blmd/dot_general | solution.py:105
  436.4 9.3 %multiply_add_fusion.2 = (bf16[2,16,32,768]{3,2,1,0:T(8,128)(2,1)}, f32[2,16,32,768]{3,2,1,0:T(8,128)}) fusion(f32[2,16,32,768]{3,2,1,0:T(8,128)S(1)} %copy-done.11, f32[768]{0:T(1024)S(1)} %copy-done.61, f32[2,768]{1,0:T(2,128)S(1)} %get-tuple-element.55, bf16[2,16,32,3072]{3,2,1,0:T(8,128)(2,1)S(1)} %bitcast.250, ...), kind=kOutput, calls=%fused_computation.103 | convolution fusion | flops 4834983936 | bytes 18883584 | tf_op jit(solution)/shard_map/blmf,fd->blmd/dot_general | solution.py:121
  465.0 10.6 %bitcast_convert_fusion.1 = bf16[768,3072]{1,0:T(8,128)(2,1)} fusion(bf16[2,16,32,3072]{3,2,1,0:T(8,128)(2,1)} %get-tuple-element.86, f32[2,16,32,768]{3,2,1,0:T(8,128)} %get-tuple-element.73, f32[2,768]{1,0:T(2,128)S(1)} %copy-done.66, f32[2,768]{1,0:T(2,128)S(1)} %get-tuple-element.53, f32[2,16,32]{2,1,0:T(8,128)S(1)} %add_rsqrt_fusion, ...), kind=kOutput, calls=%fused_computation.39 | convolution fusion | flops 4838129664 | bytes 14176256 | tf_op jit(solution)/shard_map/blmd,blmf->df/dot_general | solution.py:140
  475.6 8.5 %reshape.660 = bf16[8,384,768]{2,1,0:T(8,128)(2,1)} reshape(bf16[768,3072]{1,0:T(8,128)(2,1)} %bitcast_convert_fusion.1) | data formatting | bytes 9437184 | tf_op jit(solution)/shard_map/reshape | solution.py:338
  484.1 8.0 all-to-all-done.3
  502.9 8.1 convolution_convert_fusion.2
  513.7 6.9 multiply_reduce_fusion
  520.6 7.6 multiply_convert_fusion
  542.9 8.8 %bitcast_convert_fusion.3 = bf16[768,2304]{1,0:T(8,128)(2,1)} fusion(bf16[4,256,768]{2,1,0:T(8,128)(2,1)S(1)} %copy-done.45, bf16[4,256,768]{2,1,0:T(8,128)(2,1)} %copy.184, bf16[4,256,768]{2,1,0:T(8,128)(2,1)} %copy.183, f32[4,256,768]{2,1,0:T(8,128)} %param.21, f32[4,768]{1,0:T(4,128)S(1)} %copy-done.64, f32[4,768]{1,0:T(4,128)S(1)} %copy-done.55, ...), kind=kOutput, calls=%fused_computation.43 | convolution fusion | flops 3643736064 | bytes 11436032 | tf_op jit(solution)/shard_map/blmd,blme->de/dot_general | solution.py:104
  563.9 8.2 bitcast_convert_fusion
  572.2 6.9 pad_maximum_fusion
  579.9 11.0 %all-gather.3 = bf16[4,2,96]{2,1,0:T(2,128)(2,1)S(1)} all-gather(bf16[1,2,96]{2,1,0:T(2,128)(2,1)S(1)} %fusion.91), channel_id=1, replica_groups=mesh['grp'=4,'shard'=8] {'grp'}, dimensions={0}, use_global_device_ids=true | all-gather | bytes 1920 | tf_op jit(solution)/shard_map/all_gather | solution.py:315
  602.5 7.1 multiply_reduce_fusion.8
  613.1 18.8 %reduce-scatter.4.cloned.1.call-done = bf16[1,384,768]{2,1,0:T(8,128)(2,1)} async-done(((bf16[8,384,768]{2,1,0:T(8,128)(2,1)}), bf16[1,384,768]{2,1,0:T(8,128)(2,1)}) %reduce-scatter.4.cloned.1.call-update) | async-done | bytes 589840 | tf_op jit(solution)/shard_map/reduce_scatter | solution.py:341
  631.9 80.2 %reduce-scatter.8.cloned.1.call-done = bf16[1,768,768]{2,1,0:T(8,128)(2,1)} async-done(((bf16[8,768,768]{2,1,0:T(8,128)(2,1)}), bf16[1,768,768]{2,1,0:T(8,128)(2,1)}) %reduce-scatter.8.cloned.1.call-update) | async-done | bytes 1179664 | tf_op jit(solution)/shard_map/reduce_scatter | solution.py:341
  712.4 9.9 %all-gather.1 = f32[8,1,17664]{2,1,0:T(1,128)S(1)} all-gather(f32[1,1,17664]{2,1,0:T(1,128)S(1)} %reshape.754), channel_id=2, replica_groups=mesh['grp'=4,'shard'=8] {'shard'}, dimensions={0}, use_global_device_ids=true | all-gather | bytes 635904 | tf_op jit(solution)/shard_map/all_gather | solution.py:297
  722.9 12.3 %all-reduce = (f32[8]{0:T(128)S(1)}, f32[480]{0:T(512)S(1)}) all-reduce(f32[8]{0:T(128)S(1)} %reshape.652, f32[480]{0:T(512)S(1)} %pad_maximum_fusion.8), channel_id=1, replica_groups=mesh['grp'=4,'shard'=8] {'grp'}, use_global_device_ids=true, to_apply=%region_20.23 | all-reduce | flops 488 | bytes 3904 | tf_op jit(solution)/shard_map/psum | solution.py:322
  735.8 14.4 %all-gather.2 = bf16[4,2,6912]{2,1,0:T(2,128)(2,1)S(1)} all-gather(bf16[1,2,6912]{2,1,0:T(2,128)(2,1)S(1)} %reshape.756), channel_id=1, replica_groups=mesh['grp'=4,'shard'=8] {'grp'}, dimensions={0}, use_global_device_ids=true | all-gather | bytes 138240 | tf_op jit(solution)/shard_map/all_gather | solution.py:303
  756.8 54.6 %all-reduce.7.cloned.1.call-done = (bf16[384,768]{1,0:T(8,128)(2,1)}, bf16[384,768]{1,0:T(8,128)(2,1)}, bf16[768,768]{1,0:T(8,128)(2,1)}) async-done(((bf16[384,768]{1,0:T(8,128)(2,1)}, bf16[384,768]{1,0:T(8,128)(2,1)}, bf16[768,768]{1,0:T(8,128)(2,1)}), (bf16[384,768]{1,0:T(8,128)(2,1)}, bf16[384,768]{1,0:T(8,128)(2,1)}, bf16[768,768]{1,0:T(8,128)(2,1)})) %all-reduce.7.cloned.1.call-update) | async-done | bytes 2359312 | tf_op jit(solution)/shard_map/psum | solution.py:342
  (370 shorter events, 298.5 us)
Async XLA Ops:
  7.2 62.5 %all-reduce.5.cloned.1.call-start = ((), (), s32[]{:S(2)}) async-start(), calls=%async_computation.7 | async-start | bytes 147456 | tf_op jit(solution)/shard_map/psum | solution.py:204
  8.0 15.1 %copy-start.73 = (pred[2]{0:T(512)(128)(4,1)}, pred[2]{0:T(512)(128)(4,1)S(1)}, u32[]{:S(2)}) copy-start(pred[2]{0:T(512)(128)(4,1)S(1)} %compare_and_fusion.2) | copy-start | bytes 10
  15.7 91.0 %all-gather.11.cloned.1.call-start = ((), (), s32[]{:S(2)}) async-start(), calls=%async_computation.8 | async-start | bytes 3981312 | tf_op jit(solution)/shard_map/all_gather | solution.py:185
  16.5 121.6 %all-gather.13.cloned.1.call-start = ((), (), s32[]{:S(2)}) async-start(), calls=%async_computation.9 | async-start | bytes 1327104 | tf_op jit(solution)/shard_map/all_gather | solution.py:186
  17.2 172.6 %all-gather.15.cloned.1.call-start = ((), (), s32[]{:S(2)}) async-start(), calls=%async_computation.10 | async-start | bytes 3981312 | tf_op jit(solution)/shard_map/all_gather | solution.py:187
  17.8 227.2 %all-gather.17.cloned.1.call-start = ((), (), s32[]{:S(2)}) async-start(), calls=%async_computation.11 | async-start | bytes 1327104 | tf_op jit(solution)/shard_map/all_gather | solution.py:188
  18.4 237.0 %all-gather.19.cloned.1.call-start = ((), (), s32[]{:S(2)}) async-start(), calls=%async_computation.12 | async-start | bytes 5308416 | tf_op jit(solution)/shard_map/all_gather | solution.py:189
  24.4 120.8 %all-to-all-start.2 = ((bf16[8,4,32,768]{3,2,1,0:T(8,128)(2,1)}), bf16[8,4,32,768]{3,2,1,0:T(8,128)(2,1)}, u32[]{:S(2)}, u32[]{:S(2)}) async-start(bf16[8,4,32,768]{3,2,1,0:T(8,128)(2,1)} %copy.168), calls=%async_computation.2 | async-start | bytes 3145728 | tf_op jit(solution)/shard_map/all_to_all | solution.py:236
  32.3 81.4 %copy-start.56 = (f32[4,256]{1,0:T(4,128)}, f32[4,256]{1,0:T(4,128)S(1)}, u32[]{:S(2)}) copy-start(f32[4,256]{1,0:T(4,128)S(1)} %broadcast_multiply_fusion.8) | copy-start | bytes 12292
  34.7 79.0 %copy-start.59 = (f32[4,256]{1,0:T(4,128)}, f32[4,256]{1,0:T(4,128)S(1)}, u32[]{:S(2)}) copy-start(f32[4,256]{1,0:T(4,128)S(1)} %add_rsqrt_fusion.2) | copy-start | bytes 12292
  71.3 42.4 %copy-start.54 = (f32[4,768]{1,0:T(4,128)}, f32[4,768]{1,0:T(4,128)S(1)}, u32[]{:S(2)}) copy-start(f32[4,768]{1,0:T(4,128)S(1)} %get-tuple-element.52) | copy-start | bytes 36868
  71.3 42.4 %copy-start.63 = (f32[4,768]{1,0:T(4,128)}, f32[4,768]{1,0:T(4,128)S(1)}, u32[]{:S(2)}) copy-start(f32[4,768]{1,0:T(4,128)S(1)} %get-tuple-element.51) | copy-start | bytes 36868
  71.3 66.7 %copy-start.52 = (f32[4,768]{1,0:T(4,128)}, f32[4,768]{1,0:T(4,128)S(1)}, u32[]{:S(2)}) copy-start(f32[4,768]{1,0:T(4,128)S(1)} %get-tuple-element.50) | copy-start | bytes 36868
  145.2 34.0 %all-to-all-start = ((bf16[8,4,32,768]{3,2,1,0:T(8,128)(2,1)}), bf16[8,4,32,768]{3,2,1,0:T(8,128)(2,1)S(1)}, u32[]{:S(2)}, u32[]{:S(2)}) async-start(bf16[8,4,32,768]{3,2,1,0:T(8,128)(2,1)} %bitcast.226), calls=%async_computation | async-start | bytes 3145728 | tf_op jit(solution)/shard_map/all_to_all | solution.py:236
  148.8 153.0 %all-gather.21.cloned.1.call-start = ((), (), s32[]{:S(2)}) async-start(), calls=%async_computation.13 | async-start | bytes 5308416 | tf_op jit(solution)/shard_map/all_gather | solution.py:190
  149.5 463.6 %reduce-scatter.6.cloned.1.call-start = ((), (), s32[]{:S(2)}) async-start(), calls=%async_computation.15 | async-start | bytes 5308416 | tf_op jit(solution)/shard_map/reduce_scatter | solution.py:341
  152.9 102.4 %copy-start.65 = (f32[2,768]{1,0:T(2,128)}, f32[2,768]{1,0:T(2,128)S(1)}, u32[]{:S(2)}) copy-start(f32[2,768]{1,0:T(2,128)S(1)} %get-tuple-element.54) | copy-start | bytes 18436
  182.4 62.6 %copy-start.6 = (bf16[32,32,768]{2,1,0:T(8,128)(2,1)}, bf16[32,32,768]{2,1,0:T(8,128)(2,1)S(1)}, u32[]{:S(2)}) copy-start(bf16[32,32,768]{2,1,0:T(8,128)(2,1)S(1)} %gather_fusion.5) | copy-start | bytes 4718596
  301.8 19.7 %copy-start.10 = (f32[2,16,32,768]{3,2,1,0:T(8,128)S(1)}, f32[2,16,32,768]{3,2,1,0:T(8,128)}, u32[]{:S(2)}) copy-start(f32[2,16,32,768]{3,2,1,0:T(8,128)} %get-tuple-element.73) | copy-start | bytes 9437188
  338.0 19.4 %slice-start = ((s8[6291456]{0:T(1024)(128)(4,1)}), s8[2097152]{0:T(1024)(128)(4,1)S(1)}, s32[]{:S(2)}) async-start(s8[6291456]{0:T(1024)(128)(4,1)} %bitcast.230), calls=%async_computation.18 | async-start | bytes 4194304
  461.2 30.9 %all-to-all-start.3 = ((bf16[8,4,32,768]{3,2,1,0:T(8,128)(2,1)}), bf16[8,4,32,768]{3,2,1,0:T(8,128)(2,1)S(1)}, u32[]{:S(2)}, u32[]{:S(2)}) async-start(bf16[8,4,32,768]{3,2,1,0:T(8,128)(2,1)} %bitcast.248), calls=%async_computation.3 | async-start | bytes 3145728 | tf_op jit(solution)/shard_map/all_to_all | solution.py:241
  464.9 167.0 %reduce-scatter.4.cloned.1.call-start = ((), (), s32[]{:S(2)}) async-start(), calls=%async_computation.14 | async-start | bytes 5308416 | tf_op jit(solution)/shard_map/reduce_scatter | solution.py:341
  475.6 16.5 %copy-start.53 = (f32[4,768]{1,0:T(4,128)S(1)}, f32[4,768]{1,0:T(4,128)}, u32[]{:S(2)}) copy-start(f32[4,768]{1,0:T(4,128)} %copy-done.52) | copy-start | bytes 36868
  563.9 148.2 %reduce-scatter.8.cloned.1.call-start = ((), (), s32[]{:S(2)}) async-start(), calls=%async_computation.16 | async-start | bytes 10616832 | tf_op jit(solution)/shard_map/reduce_scatter | solution.py:341
  590.9 163.8 %all-to-all-start.1 = ((bf16[8,4,32,768]{3,2,1,0:T(8,128)(2,1)}), bf16[8,4,32,768]{3,2,1,0:T(8,128)(2,1)S(1)}, u32[]{:S(2)}, u32[]{:S(2)}) async-start(bf16[8,4,32,768]{3,2,1,0:T(8,128)(2,1)} %bitcast.32), calls=%async_computation.1 | async-start | bytes 3145728 | tf_op jit(solution)/shard_map/all_to_all | solution.py:241
  594.5 216.9 %all-reduce.7.cloned.1.call-start = ((), (), s32[]{:S(2)}) async-start(), calls=%async_computation.17 | async-start | bytes 4718592 | tf_op jit(solution)/shard_map/psum | solution.py:342
  610.1 102.0 %copy-start.69 = (f32[2,768]{1,0:T(2,128)S(1)}, f32[2,768]{1,0:T(2,128)}, u32[]{:S(2)}) copy-start(f32[2,768]{1,0:T(2,128)} %get-tuple-element.19) | copy-start | bytes 18436
  610.2 102.0 %copy-start.68 = (f32[2,768]{1,0:T(2,128)S(1)}, f32[2,768]{1,0:T(2,128)}, u32[]{:S(2)}) copy-start(f32[2,768]{1,0:T(2,128)} %get-tuple-element.26) | copy-start | bytes 18436
  610.2 102.0 %copy-start.67 = (f32[2,768]{1,0:T(2,128)S(1)}, f32[2,768]{1,0:T(2,128)}, u32[]{:S(2)}) copy-start(f32[2,768]{1,0:T(2,128)} %get-tuple-element.17) | copy-start | bytes 18436
  610.2 102.1 %copy-start.58 = (f32[768]{0:T(1024)S(1)}, f32[768]{0:T(1024)}, u32[]{:S(2)}) copy-start(f32[768]{0:T(1024)} %get-tuple-element.29) | copy-start | bytes 9220
  610.2 102.1 %copy-start.62 = (f32[3072]{0:T(1024)S(1)}, f32[3072]{0:T(1024)}, u32[]{:S(2)}) copy-start(f32[3072]{0:T(1024)} %get-tuple-element.85) | copy-start | bytes 36868
  735.2 21.6 %copy-start.78 = (f32[480]{0:T(512)}, f32[480]{0:T(512)S(1)}, u32[]{:S(2)}) copy-start(f32[480]{0:T(512)S(1)} %get-tuple-element.32) | copy-start | bytes 5764
  (66 other events, 333.5 us)
Sparse Core Ops, SparseCore 0:
  15.8 53.8 all-reduce.4
  71.6 35.0 all-gather.10
  108.6 23.9 all-gather.12
  134.3 43.2 all-gather.14
  179.3 26.2 all-gather.16
  207.3 38.7 all-gather.18
  248.0 38.7 all-gather.20
  425.5 62.7 reduce-scatter.5
  564.0 67.8 reduce-scatter.3
  635.2 76.8 reduce-scatter.7
  714.7 96.6 all-reduce.6
